TPU v7x, 128 devices: a whole 4x4x4 slice. The times are simulated.
128 devices in a mesh: fsdp: 8 (over y_lo, z), seq: 16 (over x, y_hi, core).
Axes of the slice: x: 4, y: 4 (y_hi: 2, y_lo: 2; y = y_hi * 2 + y_lo), z: 4, core: 2. Of those that a mesh axis runs over, the one named last changes fastest.
Arguments:
- tokens: bfloat16 [7168, 4096], P(('fsdp', 'seq')), may hold values from -6 to 6
- grad_out: bfloat16 [7168, 4096], P(('fsdp', 'seq')), may hold values from -6 to 6
- gate_weight: bfloat16 [4096, 14336], P('fsdp', 'seq'), may hold values from -0.09375 to 0.09375
- up_weight: bfloat16 [4096, 14336], P('fsdp', 'seq'), may hold values from -0.09375 to 0.09375
- down_weight: bfloat16 [14336, 4096], P('seq', 'fsdp'), may hold values from -0.09375 to 0.09375
- keep_mask: int32 [8, 112], P(None, 'seq'), may hold values from 0 to 1, as said below
- task_ids: int32 [7168], P('fsdp'), may hold values from 0 to 7
Outputs:
- layer_out: bfloat16 [7168, 4096], P(('fsdp', 'seq'))
- input_grad: bfloat16 [7168, 4096], P(('fsdp', 'seq'))
Inputs may be any that keep to these rules, and one draw needn't show every extreme that they name: `keep_mask`: entries are 0 or 1. In each aligned group of 7 consecutive blocks at most 4 blocks are kept by some task, and exactly 4 in at least one group; the other blocks of a group are kept by no task.
All inputs are finite; a program needn't handle non-finite values.
Results may differ from a plain program's by a relative error of at most 0.014.
Values may be sent and summed in bfloat16 or wider, within the bound.
A program may use at most 128 MiB of HBM per device.

v0:
```python
import jax
import jax.numpy as jnp
from jax import lax
from jax.sharding import PartitionSpec as P


def pick_columns(weight, chosen, block_count, block_width):
    model_width = weight.shape[0]
    shaped = weight.reshape(model_width, block_count, block_width)
    return jnp.take(shaped, chosen, axis=1).reshape(model_width, chosen.shape[0] * block_width)


def pick_rows(weight, chosen, block_count, block_width):
    columns = weight.shape[1]
    shaped = weight.reshape(block_count, block_width, columns)
    return jnp.take(shaped, chosen, axis=0).reshape(chosen.shape[0] * block_width, columns)


def transposed(left, right):
    return lax.dot_general(
        left, right, (((1,), (1,)), ((), ())), preferred_element_type=jnp.float32
    )


def local(tokens, grad_out, gate_weight, up_weight, down_weight, keep_mask, task_ids):
    token_rows, grad_rows = (
        lax.all_gather(tokens, "seq", axis=0, tiled=True),
        lax.all_gather(grad_out, "seq", axis=0, tiled=True),
    )
    task_count, block_count = keep_mask.shape
    local_width = gate_weight.shape[1]
    block_width = local_width // block_count
    kept_count = block_count * 4 // 7
    alive_blocks = jnp.max(keep_mask, axis=0)
    ranking = jnp.argsort(
        (1 - alive_blocks) * block_count + jnp.arange(block_count, dtype=jnp.int32)
    )
    chosen = ranking[:kept_count]
    keep_local = jnp.take(keep_mask, chosen, axis=1)
    gate_pick = pick_columns(gate_weight, chosen, block_count, block_width)
    up_pick = pick_columns(up_weight, chosen, block_count, block_width)
    down_pick = pick_rows(down_weight, chosen, block_count, block_width)
    gate_full, up_full = (
        lax.all_gather(gate_pick, "fsdp", axis=0, tiled=True),
        lax.all_gather(up_pick, "fsdp", axis=0, tiled=True),
    )
    down_full = lax.all_gather(down_pick, "fsdp", axis=1, tiled=True)
    onehot_tasks = (task_ids[:, None] == jnp.arange(task_count, dtype=jnp.int32)[None, :]).astype(
        jnp.float32
    )
    row_keep = jnp.dot(onehot_tasks, keep_local.astype(jnp.float32))
    neuron_mask = jnp.repeat(row_keep, block_width, axis=1)
    gate_pre = jnp.dot(token_rows, gate_full, preferred_element_type=jnp.float32)
    up_pre = jnp.dot(token_rows, up_full, preferred_element_type=jnp.float32)
    logistic = jax.nn.sigmoid(gate_pre)
    activated = gate_pre * logistic
    hidden = (activated * up_pre * neuron_mask).astype(jnp.bfloat16)
    layer_out = lax.psum_scatter(
        jnp.dot(hidden, down_full, preferred_element_type=jnp.float32).astype(jnp.bfloat16),
        "seq",
        scatter_dimension=0,
        tiled=True,
    )
    hidden_grad = transposed(grad_rows, down_full)
    masked_grad = hidden_grad * neuron_mask
    gate_grad = (masked_grad * up_pre * logistic * (1.0 + gate_pre * (1.0 - logistic))).astype(
        jnp.bfloat16
    )
    up_grad = (masked_grad * activated).astype(jnp.bfloat16)
    input_grad = lax.psum_scatter(
        (transposed(gate_grad, gate_full) + transposed(up_grad, up_full)).astype(jnp.bfloat16),
        "seq",
        scatter_dimension=0,
        tiled=True,
    )
    return (layer_out, input_grad)


def solution(mesh):
    placed = (
        P(("fsdp", "seq"), None),
        P(("fsdp", "seq"), None),
        P("fsdp", "seq"),
        P("fsdp", "seq"),
        P("seq", "fsdp"),
        P(None, "seq"),
        P("fsdp"),
    )
    return jax.shard_map(
        local,
        mesh=mesh,
        in_specs=placed,
        out_specs=(P(("fsdp", "seq"), None), P(("fsdp", "seq"), None)),
        check_vma=False,
    )
```

profile of v0, /device:TPU:0, one launch (start us, length us, event | category | flops | bytes accessed | tf_op | source)
XLA Modules:
  0.0 531.2 jit_solution(10121844740761770336)
XLA Ops:
  7.2 0.8 reduce_max.9
  8.0 1.0 sort.17
  9.0 1.5 copy.15
  11.1 1.5 copy.18
  12.6 1.3 copy.19
  13.9 0.6 gather_fusion.2
  14.5 1.8 gather_fusion.3
  16.5 1.0 copy.17
  17.6 0.7 all-gather.8.cloned.1.call-update
  18.4 1.0 copy.20
  20.2 0.9 bitcast_select_fusion
  22.9 50.1 %all-gather.6.cloned.1.call-done = bf16[4096,512]{0,1:T(8,128)(2,1)} async-done(((bf16[512,512]{0,1:T(8,128)(2,1)}), bf16[4096,512]{0,1:T(8,128)(2,1)}) %all-gather.6.cloned.1.call-update) | async-done | bytes 4194320 | tf_op jit(solution)/shard_map/all_gather | solution.py:44
  73.0 69.4 %all-gather.8.cloned.1.call-done = bf16[896,4096]{1,0:T(8,128)(2,1)} async-done(((bf16[56,4096]{1,0:T(8,128)(2,1)}), bf16[896,4096]{1,0:T(8,128)(2,1)}) %all-gather.8.cloned.1.call-update) | async-done | bytes 7340048 | tf_op jit(solution)/shard_map/all_gather | solution.py:27
  142.3 9.9 %fusion.15 = f32[512,896]{1,0:T(8,128)S(1)} fusion(bf16[4096,512]{0,1:T(8,128)(2,1)} %all-gather.6.cloned.1.call-done, bf16[896,4096]{1,0:T(8,128)(2,1)} %all-gather.8.cloned.1.call-done), kind=kOutput, calls=%fused_computation.38 | convolution fusion | flops 3758096384 | bytes 13369344 | tf_op jit(solution)/shard_map/dot_general | solution.py:53
  152.2 42.6 %all-gather.10.cloned.1.call-done = bf16[4096,512]{0,1:T(8,128)(2,1)} async-done(((bf16[512,512]{0,1:T(8,128)(2,1)}), bf16[4096,512]{0,1:T(8,128)(2,1)}) %all-gather.10.cloned.1.call-update) | async-done | bytes 4194320 | tf_op jit(solution)/shard_map/all_gather | solution.py:45
  194.8 10.1 %fusion.16 = f32[512,896]{1,0:T(8,128)} fusion(bf16[4096,512]{0,1:T(8,128)(2,1)} %all-gather.10.cloned.1.call-done, bf16[896,4096]{1,0:T(8,128)(2,1)} %all-gather.8.cloned.1.call-done), kind=kOutput, calls=%fused_computation.39 | convolution fusion | flops 3758096384 | bytes 13369344 | tf_op jit(solution)/shard_map/dot_general | solution.py:54
  204.9 42.8 %all-gather.12.cloned.1.call-done = bf16[512,4096]{1,0:T(8,128)(2,1)} async-done(((bf16[512,512]{1,0:T(8,128)(2,1)}), bf16[512,4096]{1,0:T(8,128)(2,1)}) %all-gather.12.cloned.1.call-update) | async-done | bytes 4194320 | tf_op jit(solution)/shard_map/all_gather | solution.py:47
  247.7 69.2 %all-gather.14.cloned.1.call-done = bf16[896,4096]{1,0:T(8,128)(2,1)} async-done(((bf16[56,4096]{1,0:T(8,128)(2,1)}), bf16[896,4096]{1,0:T(8,128)(2,1)}) %all-gather.14.cloned.1.call-update) | async-done | bytes 7340048 | tf_op jit(solution)/shard_map/all_gather | solution.py:28
  316.9 11.0 %multiply_convert_fusion = (bf16[896,512]{0,1:T(8,128)(2,1)}, bf16[896,512]{0,1:T(8,128)(2,1)S(1)}, bf16[896,512]{0,1:T(8,128)(2,1)S(1)}) fusion(f32[896,4]{0,1:T(4,128)S(1)} %fusion.8, f32[512,896]{1,0:T(8,128)S(1)} %fusion.15, f32[512,896]{1,0:T(8,128)} %fusion.16, bf16[512,4096]{1,0:T(8,128)(2,1)} %all-gather.12.cloned.1.call-done, ...), kind=kOutput, calls=%fused_computation.21 | convolution fusion | flops 3765895168 | bytes 17971200 | tf_op jit(solution)/shard_map/dot_general | solution.py:20
  327.9 6.2 %convolution_convert_fusion = bf16[896,4096]{1,0:T(8,128)(2,1)} fusion(bf16[896,512]{0,1:T(8,128)(2,1)S(1)} %get-tuple-element.9, bf16[512,4096]{1,0:T(8,128)(2,1)S(1)} %copy-done.2), kind=kOutput, calls=%fused_computation.5 | convolution fusion | flops 3761766400 | bytes 12451840 | tf_op jit(solution)/shard_map/dot_general | solution.py:59
  334.2 12.6 %fusion.17 = f32[896,4096]{1,0:T(8,128)} fusion(bf16[896,512]{0,1:T(8,128)(2,1)S(1)} %get-tuple-element.8, bf16[4096,512]{0,1:T(8,128)(2,1)} %all-gather.6.cloned.1.call-done), kind=kOutput, calls=%fused_computation.40 | convolution fusion | flops 3758096384 | bytes 19791872 | tf_op jit(solution)/shard_map/dot_general | solution.py:20
  346.7 10.5 %add_convert_fusion = bf16[896,4096]{1,0:T(8,128)(2,1)} fusion(f32[896,4096]{1,0:T(8,128)} %fusion.17, bf16[896,512]{0,1:T(8,128)(2,1)S(1)} %copy-done.3, bf16[4096,512]{0,1:T(8,128)(2,1)S(1)} %copy-done.5), kind=kOutput, calls=%fused_computation.4 | convolution fusion | flops 3765436416 | bytes 27131904 | tf_op jit(solution)/shard_map/dot_general | solution.py:20
  357.2 69.3 %reduce-scatter.3.cloned.1.call-done = bf16[56,4096]{1,0:T(8,128)(2,1)} async-done(((bf16[896,4096]{1,0:T(8,128)(2,1)}), bf16[56,4096]{1,0:T(8,128)(2,1)}) %reduce-scatter.3.cloned.1.call-update) | async-done | bytes 458768 | tf_op jit(solution)/shard_map/reduce_scatter | solution.py:58
  426.5 97.8 %reduce-scatter.5.cloned.1.call-done = bf16[56,4096]{1,0:T(8,128)(2,1)} async-done(((bf16[896,4096]{1,0:T(8,128)(2,1)}), bf16[56,4096]{1,0:T(8,128)(2,1)}) %reduce-scatter.5.cloned.1.call-update) | async-done | bytes 458768 | tf_op jit(solution)/shard_map/reduce_scatter | solution.py:70
  (38 shorter events, 3.5 us)
Async XLA Ops:
  7.2 12.3 %copy-start = (bf16[896,512]{1,0:T(8,128)(2,1)S(1)}, bf16[896,512]{1,0:T(8,128)(2,1)}, u32[]{:S(2)}) copy-start(bf16[896,512]{1,0:T(8,128)(2,1)} %param.13) | copy-start | bytes 2752516
  7.2 65.8 %all-gather.6.cloned.1.call-start = ((), (), s32[]{:S(2)}) async-start(), calls=%async_computation.2 | async-start | bytes 4718592 | tf_op jit(solution)/shard_map/all_gather | solution.py:44
  16.3 5.6 %copy-start.4 = (s32[8,7]{1,0:T(8,128)S(1)}, s32[8,7]{1,0:T(8,128)}, u32[]{:S(2)}) copy-start(s32[8,7]{1,0:T(8,128)} %param.14) | copy-start | bytes 676
  16.4 6.2 %copy-start.6 = (s32[896]{0:T(1024)S(1)}, s32[896]{0:T(1024)}, u32[]{:S(2)}) copy-start(s32[896]{0:T(1024)} %param.15) | copy-start | bytes 10756
  17.6 124.8 %all-gather.8.cloned.1.call-start = ((), (), s32[]{:S(2)}) async-start(), calls=%async_computation.3 | async-start | bytes 7798784 | tf_op jit(solution)/shard_map/all_gather | solution.py:27
  18.3 176.5 %all-gather.10.cloned.1.call-start = ((), (), s32[]{:S(2)}) async-start(), calls=%async_computation.4 | async-start | bytes 4718592 | tf_op jit(solution)/shard_map/all_gather | solution.py:45
  19.4 228.3 %all-gather.12.cloned.1.call-start = ((), (), s32[]{:S(2)}) async-start(), calls=%async_computation.5 | async-start | bytes 4718592 | tf_op jit(solution)/shard_map/all_gather | solution.py:47
  21.1 295.8 %all-gather.14.cloned.1.call-start = ((), (), s32[]{:S(2)}) async-start(), calls=%async_computation.7 | async-start | bytes 7798784 | tf_op jit(solution)/shard_map/all_gather | solution.py:28
  21.7 404.8 %reduce-scatter.3.cloned.1.call-start = ((), (), s32[]{:S(2)}) async-start(), calls=%async_computation.6 | async-start | bytes 7798784 | tf_op jit(solution)/shard_map/reduce_scatter | solution.py:58
  316.9 11.0 %copy-start.2 = (bf16[512,4096]{1,0:T(8,128)(2,1)S(1)}, bf16[512,4096]{1,0:T(8,128)(2,1)}, u32[]{:S(2)}) copy-start(bf16[512,4096]{1,0:T(8,128)(2,1)} %all-gather.12.cloned.1.call-done) | copy-start | bytes 12582916
  334.1 190.3 %reduce-scatter.5.cloned.1.call-start = ((), (), s32[]{:S(2)}) async-start(), calls=%async_computation.8 | async-start | bytes 7798784 | tf_op jit(solution)/shard_map/reduce_scatter | solution.py:70
  334.1 12.6 %copy-start.3 = (bf16[896,512]{0,1:T(8,128)(2,1)S(1)}, bf16[896,512]{0,1:T(8,128)(2,1)}, u32[]{:S(2)}) copy-start(bf16[896,512]{0,1:T(8,128)(2,1)} %get-tuple-element.7) | copy-start | bytes 2752516
  334.2 12.6 %copy-start.5 = (bf16[4096,512]{0,1:T(8,128)(2,1)S(1)}, bf16[4096,512]{0,1:T(8,128)(2,1)}, u32[]{:S(2)}) copy-start(bf16[4096,512]{0,1:T(8,128)(2,1)} %all-gather.10.cloned.1.call-done) | copy-start | bytes 12582916
  346.7 177.7 %copy-start.1 = (bf16[896,512]{1,0:T(8,128)(2,1)S(1)}, bf16[896,512]{1,0:T(8,128)(2,1)}, u32[]{:S(2)}) copy-start(bf16[896,512]{1,0:T(8,128)(2,1)} %param.13) | copy-start | bytes 2752516
Sparse Core Ops, SparseCore 0:
  17.7 55.2 all-gather.5
  75.4 66.9 all-gather.7
  144.0 50.7 all-gather.9
  196.3 51.3 all-gather.11
  249.9 66.9 all-gather.13
  334.2 92.2 reduce-scatter.2
  431.3 93.0 reduce-scatter.4
where the time goes:
time: 531 us
  waiting for transfers between devices  442 us (83%)
  matrix products  60.5 us (11%)
  between operations  14.3 us (3%)
  local copies, waits for them, and re-layouts  10.7 us (2%)
    reduce_scatter x1, waiting for transfers between devices, local(): lax.psum_scatter((transposed(gate_grad, gate_full) + transposed(up_grad,...  97.8 us
    all_gather x1, waiting for transfers between devices, local(): lax.all_gather(tokens, 'seq', axis=0, tiled=True)  69.4 us
    reduce_scatter x1, waiting for transfers between devices, local(): lax.psum_scatter(jnp.dot(hidden, down_full, preferred_element_type=jnp.fl...  69.3 us
    all_gather x1, waiting for transfers between devices, local(): lax.all_gather(grad_out, 'seq', axis=0, tiled=True)  69.2 us
    all_gather x1, waiting for transfers between devices, local(): lax.all_gather(gate_pick, 'fsdp', axis=0, tiled=True)  50.1 us
    all_gather x1, waiting for transfers between devices, local(): down_full = lax.all_gather(down_pick, 'fsdp', axis=1, tiled=True)  42.8 us
    all_gather x1, waiting for transfers between devices, local(): lax.all_gather(up_pick, 'fsdp', axis=0, tiled=True)  42.6 us
    dot_general x3, matrix products, transposed(): lax.dot_general(left, right, (((1,), (1,)), ((), ())), preferred_element_...  34 us
  transfers between devices with their start and end apart: 7, of which 7 were waited for; matrix products, arithmetic and copies ran while one was open for 9% of the time, Pallas kernels for 0%

commit v1 on v0

v1 whole, which is shorter than its diff:
```python
import functools

import jax
import jax.numpy as jnp
from jax import lax
from jax.experimental import pallas as pl
from jax.experimental.pallas import tpu as pltpu
from jax.sharding import PartitionSpec as P

MESH = pl.DeviceIdType.MESH
F32, BF16 = jnp.float32, jnp.bfloat16
RING, PAIRS, SLOTS = 4, 4, 8
KEPT, BLOCK, TASKS = 4, 128, 8
TOK, GRAD, GATE, UP, DOWN = range(5)
BY_PAIR = (GATE, UP, DOWN)


def dot(left, right):
    return jnp.dot(left, right, preferred_element_type=F32)


def dot_t(left, right):
    return lax.dot_general(left, right, (((1,), (1,)), ((), ())), preferred_element_type=F32)


def kernel(
    keep_ref, tok_ref, grad_ref, gate_ref, up_ref, down_ref, onehot_ref, out_ref, ig_ref,
    rows_buf, w_buf, cols_stage, rows_stage, keep_buf, acc, hid, gate_g, up_g, part, inbox,
    local_sem, send_sem, recv_sem, core_send, core_recv, rs_send, rs_recv,
):
    f, s = lax.axis_index("fsdp"), lax.axis_index("seq")
    z, yl = f % RING, f // RING
    x, yh, core = s // 4, (s // 2) % 2, s % 2
    x_up = {"seq": ((x + 1) % RING) * 4 + yh * 2 + core}
    x_down = {"seq": ((x + RING - 1) % RING) * 4 + yh * 2 + core}
    y_far = {"seq": x * 4 + (1 - yh) * 2 + core}
    sibling = {"seq": x * 4 + yh * 2 + 1 - core}
    z_up = {"fsdp": yl * RING + (z + 1) % RING}
    z_down = {"fsdp": yl * RING + (z + RING - 1) % RING}
    y_near = {"fsdp": (1 - yl) * RING + z}

    width = w_buf.shape[-1]
    chunk = tok_ref.shape[0]
    n_rows = SLOTS * chunk

    def owner(k):
        offset = (0, 0, 1, RING - 1, 1, RING - 1, 2, 2)[k]
        other = k in (1, 4, 5, 7)
        return ((1 - yl) if other else yl) * RING + (z + offset) % RING

    def columns(k):
        return pl.ds(pl.multiple_of(owner(k) * width, width), width)

    def slot(array, k):
        if array in (TOK, GRAD):
            return rows_buf.at[array, k]
        return w_buf.at[array - GATE, 0, k]

    def neighbours(array):
        return (x_up, x_down, y_far) if array in (TOK, GRAD) else (z_up, z_down, y_near)

    sent = []

    def send(src, dst, ssem, rsem, device):
        copy = pltpu.make_async_remote_copy(
            src_ref=src, dst_ref=dst, send_sem=ssem, recv_sem=rsem, device_id=device,
            device_id_type=MESH,
        )
        copy.start()
        sent.append(copy)

    def arrived(dst, rsem, device):
        pltpu.make_async_remote_copy(
            src_ref=dst, dst_ref=dst, send_sem=local_sem.at[0], recv_sem=rsem, device_id=device,
            device_id_type=MESH,
        ).wait_recv()

    half = width // 2

    def part_of(ref, which):
        return ref if which is None else ref.at[pl.ds(which * half, half)]

    def spread(array, k, lane, to, which=None, src=None, hop=None):
        source = slot(array, k) if src is None else src
        send(
            part_of(source, which), part_of(slot(array, to), which), send_sem.at[array, lane],
            recv_sem.at[array, to if which in (None, 0) else SLOTS + to - 6], neighbours(array)[hop],
        )

    def got(array, k, which=None):
        hop = (None, 2, 0, 1, 0, 1, 1, 1)[k]
        if which is not None:
            hop = (1, 0)[which] if k == 6 else 2
        sem = recv_sem.at[array, k if which in (None, 0) else SLOTS + k - 6]
        arrived(part_of(slot(array, k), which), sem, neighbours(array)[hop])

    def to_sibling(array, k):
        w = array - GATE
        send(w_buf.at[w, 0, k], w_buf.at[w, 1, k], core_send.at[w, k], core_recv.at[w, k], sibling)

    def from_sibling(array, k):
        w = array - GATE
        arrived(w_buf.at[w, 1, k], core_recv.at[w, k], sibling)

    def first(array, src=None):
        spread(array, 0, 0, 1, src=src, hop=2)
        spread(array, 0, 1, 3, src=src, hop=0)
        spread(array, 0, 2, 2, src=src, hop=1)
        if array >= GATE:
            to_sibling(array, 0)

    def second(array):
        got(array, 1)
        spread(array, 1, 3, 5, hop=0)
        spread(array, 1, 4, 4, hop=1)
        if array >= GATE:
            to_sibling(array, 1)

    def third(array):
        got(array, 3)
        if array in BY_PAIR:
            spread(array, 3, 5, 6, which=0, hop=0)
        else:
            spread(array, 3, 5, 6, hop=0)
        if array >= GATE:
            to_sibling(array, 3)
        got(array, 2)
        if array in BY_PAIR:
            spread(array, 2, 6, 6, which=1, hop=1)
        if array >= GATE:
            to_sibling(array, 2)

    def fourth(array):
        got(array, 4)
        if array not in BY_PAIR:
            spread(array, 4, 6, 7, hop=1)
        got(array, 5)
        if array >= GATE:
            to_sibling(array, 4)
            to_sibling(array, 5)

    def fifth(array):
        if array in BY_PAIR:
            got(array, 6, 0)
            spread(array, 6, 7, 7, which=0, hop=2)
            got(array, 6, 1)
            spread(array, 6, 8, 7, which=1, hop=2)
        else:
            got(array, 6)
        if array >= GATE:
            to_sibling(array, 6)

    def sixth(array):
        if array in BY_PAIR:
            got(array, 7, 0)
            got(array, 7, 1)
        else:
            hop = neighbours(array)[0]
            arrived(slot(array, 7), recv_sem.at[array, 7], hop)
        if array >= GATE:
            to_sibling(array, 7)

    barrier = pltpu.get_barrier_semaphore()
    around = (x_up, x_down, y_far, sibling, z_up, z_down, y_near)
    for device in around:
        pl.semaphore_signal(barrier, inc=1, device_id=device, device_id_type=MESH)
    stage = (
        pltpu.make_async_copy(gate_ref, cols_stage.at[0], local_sem.at[1]),
        pltpu.make_async_copy(up_ref, cols_stage.at[1], local_sem.at[2]),
        pltpu.make_async_copy(down_ref, rows_stage, local_sem.at[3]),
        pltpu.make_async_copy(tok_ref, rows_buf.at[TOK, 0], local_sem.at[4]),
        pltpu.make_async_copy(grad_ref, rows_buf.at[GRAD, 0], local_sem.at[5]),
    )
    for copy in stage:
        copy.start()

    n_blocks = keep_ref.shape[1]
    spare = n_blocks - KEPT
    alive = []
    for b in range(n_blocks):
        seen = keep_ref[0, b]
        for t in range(1, TASKS):
            seen = jnp.maximum(seen, keep_ref[t, b])
        alive.append(seen)
    room = KEPT - sum(alive[1:], alive[0])
    taken, place, before = [], [], jnp.int32(0)
    for b in range(n_blocks):
        fill = (1 - alive[b]) * jnp.where(room > 0, 1, 0)
        room = room - fill
        taken.append(alive[b] + fill)
        place.append(before)
        before = before + taken[b]
    picks = [
        [(b, taken[b] * jnp.where(place[b] == j, 1, 0)) for b in range(j, j + spare + 1)]
        for j in range(KEPT)
    ]

    pl.semaphore_wait(barrier, len(around))
    first(TOK, tok_ref)

    def blend(terms, shape):
        blend_of = None
        for take, block in terms:
            term = block * jnp.full(shape, take.astype(F32)).astype(BF16)
            blend_of = term if blend_of is None else blend_of + term
        return blend_of

    def pack_columns(array):
        w = array - GATE
        stage[w].wait()
        step = 64

        @pl.loop(0, w_buf.shape[3] // step)
        def _(i):
            at = pl.ds(pl.multiple_of(i * step, step), step)
            for j in range(KEPT):
                terms = [(take, cols_stage[w, at, b * BLOCK : (b + 1) * BLOCK]) for b, take in picks[j]]
                w_buf[w, 0, 0, at, j * BLOCK : (j + 1) * BLOCK] = blend(terms, (step, BLOCK))

    pack_columns(GATE)
    pack_columns(UP)
    stage[2].wait()
    step = 32

    @pl.loop(0, BLOCK // step)
    def _(i):
        for j in range(KEPT):
            terms = [
                (take, rows_stage[pl.ds(pl.multiple_of(b * BLOCK + i * step, step), step), :])
                for b, take in picks[j]
            ]
            at = pl.ds(pl.multiple_of(j * BLOCK + i * step, step), step)
            w_buf[2, 0, 0, at, :] = blend(terms, (step, width))

    task_row = lax.broadcasted_iota(jnp.int32, (keep_buf.shape[1], BLOCK), 0)
    for j in range(KEPT):
        block = jnp.zeros((keep_buf.shape[1], BLOCK), F32)
        for t in range(TASKS):
            kept = sum(take * keep_ref[t, b] for b, take in picks[j])
            block = jnp.where(task_row == t, kept.astype(F32), block)
        keep_buf[0, :, j * BLOCK : (j + 1) * BLOCK] = block.astype(BF16)

    first(GATE)
    first(UP)
    first(GRAD, grad_ref)
    send(keep_buf.at[0], keep_buf.at[1], core_send.at[3, 0], core_recv.at[3, 0], sibling)
    stage[3].wait()
    stage[4].wait()

    second(TOK)
    second(GATE)
    third(GATE)
    second(UP)
    third(TOK)
    third(UP)
    second(GRAD)
    first(DOWN)
    fourth(TOK)
    fourth(GATE)
    third(GRAD)
    fifth(TOK)
    sixth(TOK)

    def rows(array, k):
        return rows_buf[array, :, :, columns(k)].reshape(n_rows, width)

    def group(c):
        return pl.ds(pl.multiple_of(c * width, width), width)

    def forward(j):
        a, b = 2 * j, 2 * j + 1
        for array in (GATE, UP):
            from_sibling(array, a)
            from_sibling(array, b)

        @pl.loop(0, 2)
        def _(c):
            for w in range(2):
                new = dot(rows(TOK, a), w_buf[w, c, a]) + dot(rows(TOK, b), w_buf[w, c, b])
                if j:
                    new = acc[w, :, group(c)] + new
                acc[w, :, group(c)] = new

    def backward(j):
        a, b = 2 * j, 2 * j + 1

        @pl.loop(0, 2)
        def _(c):
            new = dot_t(rows(GRAD, a), w_buf[2, c, a]) + dot_t(rows(GRAD, b), w_buf[2, c, b])
            if j:
                new = acc[2, :, group(c)] + new
            acc[2, :, group(c)] = new

    def activate():
        step = 32

        @pl.loop(0, n_rows // step)
        def _(i):
            at = pl.ds(pl.multiple_of(i * step, step), step)
            for c in range(2):
                cols = slice(c * width, (c + 1) * width)
                mask = dot(onehot_ref[at, :], keep_buf[c])
                gate_pre, up_pre = acc[0, at, cols], acc[1, at, cols]
                logistic = jax.nn.sigmoid(gate_pre)
                activated = gate_pre * logistic * mask
                hid[at, cols] = (activated * up_pre).astype(BF16)
                acc[0, at, cols] = mask * up_pre * logistic * (1.0 + gate_pre * (1.0 - logistic))
                acc[1, at, cols] = activated

    def pull_back():
        step = 32

        @pl.loop(0, n_rows // step)
        def _(i):
            at = pl.ds(pl.multiple_of(i * step, step), step)
            hidden_grad = acc[2, at, :]
            gate_g[at, :] = (hidden_grad * acc[0, at, :]).astype(BF16)
            up_g[at, :] = (hidden_grad * acc[1, at, :]).astype(BF16)

    def out_part(j):
        @pl.loop(2 * j, 2 * j + 2)
        def _(k):
            new = dot(hid[:, :width], w_buf[2, 0, k]) + dot(hid[:, width:], w_buf[2, 1, k])
            part[0, k] = new.reshape(SLOTS, chunk, width).astype(BF16)

    def grad_part(j):
        @pl.loop(2 * j, 2 * j + 2)
        def _(k):
            new = dot_t(gate_g[:, :width], w_buf[0, 0, k]) + dot_t(gate_g[:, width:], w_buf[0, 1, k])
            new += dot_t(up_g[:, :width], w_buf[1, 0, k]) + dot_t(up_g[:, width:], w_buf[1, 1, k])
            part[1, k] = new.reshape(SLOTS, chunk, width).astype(BF16)

    def piece(o, j, at):
        return part.at[o, pl.ds(2 * j, 2), at]

    def post(o, j, at, m, device):
        send(piece(o, j, at), inbox.at[o, j, m], rs_send.at[o, j, m], rs_recv.at[o, j, m], device)

    def collect(o, j, m):
        device = (x_down, x_up, x_down, x_up, x_down, x_up, y_far)[m]
        arrived(inbox.at[o, j, m], rs_recv.at[o, j, m], device)

    def sum_a(o, j):
        post(o, j, 6, 0, x_up)
        post(o, j, 7, 1, x_down)
        post(o, j, 4, 2, x_up)
        post(o, j, 3, 3, x_down)

    def sum_b(o, j):
        for m, at, device in ((0, 2, x_up), (1, 5, x_down)):
            collect(o, j, m)
            for i in range(2):
                both = part[o, 2 * j + i, at].astype(F32) + inbox[o, j, m, i].astype(F32)
                part[o, 2 * j + i, at] = both.astype(BF16)
            post(o, j, at, 4 + m, device)

    def sum_c(o, j):
        for m in (2, 3, 4, 5):
            collect(o, j, m)
        for i in range(2):
            both = part[o, 2 * j + i, 1].astype(F32) + inbox[o, j, 2, i].astype(F32)
            part[o, 2 * j + i, 1] = (both + inbox[o, j, 5, i].astype(F32)).astype(BF16)
        post(o, j, 1, 6, y_far)

    def sum_d(o, j):
        collect(o, j, 6)
        result = out_ref if o == 0 else ig_ref
        for i in range(2):
            both = part[o, 2 * j + i, 0].astype(F32) + inbox[o, j, 3, i].astype(F32)
            both = both + inbox[o, j, 4, i].astype(F32)
            result[:, columns(2 * j + i)] = (both + inbox[o, j, 6, i].astype(F32)).astype(BF16)

    forward(0)
    second(DOWN)
    forward(1)
    fourth(GRAD)
    fourth(UP)
    third(DOWN)
    fifth(GATE)
    forward(2)
    fifth(GRAD)
    sixth(GRAD)
    fifth(UP)
    sixth(GATE)
    sixth(UP)
    forward(3)
    arrived(keep_buf.at[1], core_recv.at[3, 0], sibling)
    activate()
    from_sibling(DOWN, 0)
    from_sibling(DOWN, 1)
    out_part(0)
    sum_a(0, 0)
    backward(0)
    from_sibling(DOWN, 2)
    from_sibling(DOWN, 3)
    out_part(1)
    sum_a(0, 1)
    sum_b(0, 0)
    backward(1)
    fourth(DOWN)
    from_sibling(DOWN, 4)
    from_sibling(DOWN, 5)
    out_part(2)
    sum_a(0, 2)
    sum_b(0, 1)
    sum_c(0, 0)
    backward(2)
    fifth(DOWN)
    sum_b(0, 2)
    sum_c(0, 1)
    sum_d(0, 0)
    sixth(DOWN)
    from_sibling(DOWN, 6)
    from_sibling(DOWN, 7)
    backward(3)
    pull_back()
    grad_part(0)
    sum_a(1, 0)
    out_part(3)
    sum_a(0, 3)
    sum_c(0, 2)
    sum_d(0, 1)
    grad_part(1)
    sum_a(1, 1)
    sum_b(1, 0)
    sum_b(0, 3)
    grad_part(2)
    sum_a(1, 2)
    sum_b(1, 1)
    sum_c(1, 0)
    sum_d(0, 2)
    grad_part(3)
    sum_a(1, 3)
    sum_c(0, 3)
    sum_b(1, 2)
    sum_c(1, 1)
    sum_d(1, 0)
    sum_d(0, 3)
    sum_b(1, 3)
    sum_c(1, 2)
    sum_d(1, 1)
    sum_c(1, 3)
    sum_d(1, 2)
    sum_d(1, 3)
    for copy in sent:
        copy.wait_send()


def local(tokens, grad_out, gate_weight, up_weight, down_weight, keep_mask, task_ids):
    chunk, model = tokens.shape
    depth, hidden = gate_weight.shape
    width = KEPT * BLOCK
    s = lax.axis_index("seq")
    x, yh, core = s // 4, (s // 2) % 2, s % 2
    offset = jnp.array([0, 0, 1, 3, 1, 3, 2, 2], jnp.int32)
    other = jnp.array([0, 1, 0, 0, 1, 1, 0, 1], jnp.int32)
    owners = ((x + offset) % RING) * 4 + ((yh + other) % 2) * 2 + core
    tasks = jnp.take(task_ids.reshape(2 * SLOTS, chunk), owners, axis=0)
    padded = 2 * TASKS
    onehot = (tasks[:, :, None] == jnp.arange(padded, dtype=jnp.int32)).astype(BF16)
    onehot = onehot.reshape(SLOTS * chunk, padded)
    n_rows = SLOTS * chunk
    any_space, vmem = pl.BlockSpec(memory_space=pl.ANY), pl.BlockSpec(memory_space=pltpu.VMEM)
    dma = pltpu.SemaphoreType.DMA
    return pl.pallas_call(
        kernel,
        out_shape=[jax.ShapeDtypeStruct((chunk, model), BF16)] * 2,
        in_specs=[pl.BlockSpec(memory_space=pltpu.SMEM)] + [any_space] * 5 + [vmem],
        out_specs=[vmem, vmem],
        scratch_shapes=[
            pltpu.VMEM((2, SLOTS, chunk, model), BF16),
            pltpu.VMEM((3, 2, SLOTS, depth, width), BF16),
            pltpu.VMEM((2, depth, hidden), BF16),
            pltpu.VMEM((hidden, depth), BF16),
            pltpu.VMEM((2, padded, width), BF16),
            pltpu.VMEM((3, n_rows, 2 * width), F32),
            pltpu.VMEM((n_rows, 2 * width), BF16),
            pltpu.VMEM((n_rows, 2 * width), BF16),
            pltpu.VMEM((n_rows, 2 * width), BF16),
            pltpu.VMEM((2, SLOTS, SLOTS, chunk, width), BF16),
            pltpu.VMEM((2, PAIRS, 7, 2, chunk, width), BF16),
            dma((6,)),
            dma((5, 9)),
            dma((5, SLOTS + 2)),
            dma((4, SLOTS)),
            dma((4, SLOTS)),
            dma((2, PAIRS, 7)),
            dma((2, PAIRS, 7)),
        ],
        compiler_params=pltpu.CompilerParams(
            collective_id=0, has_side_effects=True, vmem_limit_bytes=64_000_000
        ),
        name="swiglu",
    )(keep_mask, tokens, grad_out, gate_weight, up_weight, down_weight, onehot)


def solution(mesh):
    placed = (
        P(("fsdp", "seq"), None),
        P(("fsdp", "seq"), None),
        P("fsdp", "seq"),
        P("fsdp", "seq"),
        P("seq", "fsdp"),
        P(None, "seq"),
        P("fsdp"),
    )
    return jax.shard_map(
        local,
        mesh=mesh,
        in_specs=placed,
        out_specs=(P(("fsdp", "seq"), None), P(("fsdp", "seq"), None)),
        check_vma=False,
    )
```

time: 531 us -> 196 us (0.37)
  waiting for transfers between devices: 442 us -> 0 us
  Pallas kernels: 0 us -> 189 us
  matrix products: 60.5 us -> 0 us
  between operations: 14.3 us -> 0.73 us
  local copies, waits for them, and re-layouts: 10.7 us -> 4.68 us
    all_gather x5 -> x0, waiting for transfers between devices: 274 us -> none  [the longest x1 69.4 us: local(): lax.all_gather(tokens, 'seq', axis=0, tiled=True)]
    pallas_call x0 -> x1, Pallas kernels: none -> 189 us  [local(): pl.pallas_call(kernel, out_shape=[jax.ShapeDtypeStruct((chunk, model), BF...]
    reduce_scatter x2 -> x0, waiting for transfers between devices: 167 us -> none  [the longest x1 97.8 us: local(): lax.psum_scatter((transposed(gate_grad, gate_full) + transposed(up_grad,...]
    dot_general x7 -> x0, matrix products: 60.5 us -> none  [the longest x3 34 us: transposed(): lax.dot_general(left, right, (((1,), (1,)), ((), ())), preferred_element_...]
  transfers between devices with their start and end apart: 7 -> 0, of which waited for: 7 -> 0; matrix products, arithmetic and copies ran while one was open for 9% -> 0% of each run, Pallas kernels for 0% -> 0%
where the time goes in v1:
time: 196 us
  Pallas kernels  189 us (96%)
  local copies, waits for them, and re-layouts  4.68 us (2%)
    pallas_call x1, Pallas kernels, local(): pl.pallas_call(kernel, out_shape=[jax.ShapeDtypeStruct((chunk, model), BF...  189 us
    unnamed x10, local copies, waits for them, and re-layouts  3.96 us

profile of v1, /device:TPU:0, one launch (start us, length us, event | category | flops | bytes accessed | tf_op | source)
XLA Modules:
  0.0 195.8 jit_solution(11286031189823016589)
XLA Ops:
  0.7 0.0 copy-start.2
  0.7 0.0 copy-start.3
  0.7 0.6 copy-done.2
  1.3 0.0 copy-done.3
  1.4 0.0 copy-start.1
  1.4 0.7 copy-done.1
  2.1 0.1 reshape.32
  2.1 0.6 gather_fusion
  2.7 0.1 broadcast_select_fusion
  2.8 0.1 select_n.52
  2.9 0.8 fusion.onehot_ref
  3.6 189.5 %swiglu.1 = (bf16[56,4096]{1,0:T(8,128)(2,1)}, bf16[56,4096]{1,0:T(8,128)(2,1)}) custom-call(s32[8,7]{1,0:T(8,128)} %keep_ref.1, bf16[56,4096]{1,0:T(8,128)(2,1)} %tok_ref.1, bf16[56,4096]{1,0:T(8,128)(2,1)} %grad_ref.1, bf16[512,896]{1,0:T(8,128)(2,1)} %gate_ref.1, bf16[512,896]{1,0:T(8,128)(2,1)} %up_ref.1, bf16[896,512]{1,0:T(8,128)(2,1)} %down_ref.1, ...), custom_call_target="tpu_custom_call" | custom-call | tf_op jit(solution)/shard_map/swiglu/pallas_call | solution.py:465
  193.1 0.0 copy-start
  193.1 1.9 copy.13
  195.0 0.0 copy-done
  195.0 0.8 copy.14
  (2 shorter events, 0.0 us)
Async XLA Ops:
  0.7 0.7 copy-start.2
  0.7 0.7 copy-start.3
  1.4 0.7 copy-start.1
  193.1 1.9 copy-start

commit v2 on v1

--- a/solution.py
+++ b/solution.py
@@ -12,7 +12,8 @@
 RING, PAIRS, SLOTS = 4, 4, 8
 KEPT, BLOCK, TASKS = 4, 128, 8
 TOK, GRAD, GATE, UP, DOWN = range(5)
-BY_PAIR = (GATE, UP, DOWN)
+BY_PAIR = (GATE,)
+PAIR_FIRST = ((0, 3), (1, 1))
 
 
 def dot(left, right):
@@ -59,7 +60,7 @@
     def neighbours(array):
         return (x_up, x_down, y_far) if array in (TOK, GRAD) else (z_up, z_down, y_near)
 
-    sent = []
+    sent, seen_halves, lanes = [], set(), [0] * 5
 
     def send(src, dst, ssem, rsem, device):
         copy = pltpu.make_async_remote_copy(
@@ -75,24 +76,21 @@
             device_id_type=MESH,
         ).wait_recv()
 
-    half = width // 2
-
-    def part_of(ref, which):
-        return ref if which is None else ref.at[pl.ds(which * half, half)]
-
-    def spread(array, k, lane, to, which=None, src=None, hop=None):
+    def half_of(array, ref, h):
+        if array in (TOK, GRAD):
+            return ref.at[:, pl.ds(h * (ref.shape[1] // 2), ref.shape[1] // 2)]
+        return ref.at[pl.ds(h * (ref.shape[0] // 2), ref.shape[0] // 2)]
+
+    UPWARD, DOWNWARD, ACROSS = range(3)
+
+    def move(array, k, h, hop, to, src=None):
         source = slot(array, k) if src is None else src
+        lane = lanes[array]
+        lanes[array] += 1
         send(
-            part_of(source, which), part_of(slot(array, to), which), send_sem.at[array, lane],
-            recv_sem.at[array, to if which in (None, 0) else SLOTS + to - 6], neighbours(array)[hop],
+            half_of(array, source, h), half_of(array, slot(array, to), h), send_sem.at[array, lane],
+            recv_sem.at[array, 2 * to + h], neighbours(array)[hop],
         )
-
-    def got(array, k, which=None):
-        hop = (None, 2, 0, 1, 0, 1, 1, 1)[k]
-        if which is not None:
-            hop = (1, 0)[which] if k == 6 else 2
-        sem = recv_sem.at[array, k if which in (None, 0) else SLOTS + k - 6]
-        arrived(part_of(slot(array, k), which), sem, neighbours(array)[hop])
 
     def to_sibling(array, k):
         w = array - GATE
@@ -102,63 +100,47 @@
         w = array - GATE
         arrived(w_buf.at[w, 1, k], core_recv.at[w, k], sibling)
 
-    def first(array, src=None):
-        spread(array, 0, 0, 1, src=src, hop=2)
-        spread(array, 0, 1, 3, src=src, hop=0)
-        spread(array, 0, 2, 2, src=src, hop=1)
+    def need(array, k, h=None):
+        for half in (0, 1) if h is None else (h,):
+            if (array, k, half) in seen_halves:
+                continue
+            arrived(half_of(array, slot(array, k), half), recv_sem.at[array, 2 * k + half], sibling)
+            seen_halves.add((array, k, half))
+            if array >= GATE and (array, k, 1 - half) in seen_halves:
+                to_sibling(array, k)
+
+    def start(array, src=None):
+        for h in (0, 1):
+            move(array, 0, h, ACROSS, 1, src)
+            move(array, 0, h, UPWARD, 3, src)
+            move(array, 0, 1 - h, DOWNWARD, 2, src)
         if array >= GATE:
             to_sibling(array, 0)
 
     def second(array):
-        got(array, 1)
-        spread(array, 1, 3, 5, hop=0)
-        spread(array, 1, 4, 4, hop=1)
-        if array >= GATE:
-            to_sibling(array, 1)
-
-    def third(array):
-        got(array, 3)
+        need(array, 1, 0)
+        move(array, 1, 0, UPWARD, 5)
+        need(array, 1, 1)
+        move(array, 1, 1, DOWNWARD, 4)
+        move(array, 1, 1, UPWARD, 5)
+        move(array, 1, 0, DOWNWARD, 4)
+
+    def relay_own(array):
+        need(array, 3, 0)
+        move(array, 3, 0, UPWARD, 6)
+        need(array, 2, 1)
+        move(array, 2, 1, DOWNWARD, 6)
+
+    def relay_other(array):
         if array in BY_PAIR:
-            spread(array, 3, 5, 6, which=0, hop=0)
+            for h in (0, 1):
+                need(array, 6, h)
+                move(array, 6, h, ACROSS, 7)
         else:
-            spread(array, 3, 5, 6, hop=0)
-        if array >= GATE:
-            to_sibling(array, 3)
-        got(array, 2)
-        if array in BY_PAIR:
-            spread(array, 2, 6, 6, which=1, hop=1)
-        if array >= GATE:
-            to_sibling(array, 2)
-
-    def fourth(array):
-        got(array, 4)
-        if array not in BY_PAIR:
-            spread(array, 4, 6, 7, hop=1)
-        got(array, 5)
-        if array >= GATE:
-            to_sibling(array, 4)
-            to_sibling(array, 5)
-
-    def fifth(array):
-        if array in BY_PAIR:
-            got(array, 6, 0)
-            spread(array, 6, 7, 7, which=0, hop=2)
-            got(array, 6, 1)
-            spread(array, 6, 8, 7, which=1, hop=2)
-        else:
-            got(array, 6)
-        if array >= GATE:
-            to_sibling(array, 6)
-
-    def sixth(array):
-        if array in BY_PAIR:
-            got(array, 7, 0)
-            got(array, 7, 1)
-        else:
-            hop = neighbours(array)[0]
-            arrived(slot(array, 7), recv_sem.at[array, 7], hop)
-        if array >= GATE:
-            to_sibling(array, 7)
+            need(array, 5, 0)
+            move(array, 5, 0, UPWARD, 7)
+            need(array, 4, 1)
+            move(array, 4, 1, DOWNWARD, 7)
 
     barrier = pltpu.get_barrier_semaphore()
     around = (x_up, x_down, y_far, sibling, z_up, z_down, y_near)
@@ -196,7 +178,7 @@
     ]
 
     pl.semaphore_wait(barrier, len(around))
-    first(TOK, tok_ref)
+    start(TOK, tok_ref)
 
     def blend(terms, shape):
         blend_of = None
@@ -218,7 +200,10 @@
                 w_buf[w, 0, 0, at, j * BLOCK : (j + 1) * BLOCK] = blend(terms, (step, BLOCK))
 
     pack_columns(GATE)
+    start(GATE)
     pack_columns(UP)
+    start(UP)
+    start(GRAD, grad_ref)
     stage[2].wait()
     step = 32
 
@@ -240,27 +225,10 @@
             block = jnp.where(task_row == t, kept.astype(F32), block)
         keep_buf[0, :, j * BLOCK : (j + 1) * BLOCK] = block.astype(BF16)
 
-    first(GATE)
-    first(UP)
-    first(GRAD, grad_ref)
     send(keep_buf.at[0], keep_buf.at[1], core_send.at[3, 0], core_recv.at[3, 0], sibling)
     stage[3].wait()
     stage[4].wait()
 
-    second(TOK)
-    second(GATE)
-    third(GATE)
-    second(UP)
-    third(TOK)
-    third(UP)
-    second(GRAD)
-    first(DOWN)
-    fourth(TOK)
-    fourth(GATE)
-    third(GRAD)
-    fifth(TOK)
-    sixth(TOK)
-
     def rows(array, k):
         return rows_buf[array, :, :, columns(k)].reshape(n_rows, width)
 
@@ -269,6 +237,10 @@
 
     def forward(j):
         a, b = 2 * j, 2 * j + 1
+        for array in (GATE, UP):
+            for k in (a, b):
+                if k:
+                    need(array, k)
         for array in (GATE, UP):
             from_sibling(array, a)
             from_sibling(array, b)
@@ -317,6 +289,13 @@
             gate_g[at, :] = (hidden_grad * acc[0, at, :]).astype(BF16)
             up_g[at, :] = (hidden_grad * acc[1, at, :]).astype(BF16)
 
+    def ready(j):
+        for k in (2 * j, 2 * j + 1):
+            if k:
+                need(DOWN, k)
+        for k in (2 * j, 2 * j + 1):
+            from_sibling(DOWN, k)
+
     def out_part(j):
         @pl.loop(2 * j, 2 * j + 2)
         def _(k):
@@ -337,24 +316,57 @@
         send(piece(o, j, at), inbox.at[o, j, m], rs_send.at[o, j, m], rs_recv.at[o, j, m], device)
 
     def collect(o, j, m):
-        device = (x_down, x_up, x_down, x_up, x_down, x_up, y_far)[m]
-        arrived(inbox.at[o, j, m], rs_recv.at[o, j, m], device)
+        arrived(inbox.at[o, j, m], rs_recv.at[o, j, m], sibling)
+
+    def add(o, j, at, m, i):
+        both = part[o, 2 * j + i, at].astype(F32) + inbox[o, j, m, i].astype(F32)
+        part[o, 2 * j + i, at] = both.astype(BF16)
+
+    def finish(o, j, terms):
+        result = out_ref if o == 0 else ig_ref
+        for i in range(2):
+            both = part[o, 2 * j + i, 0].astype(F32)
+            for m in terms:
+                both = both + inbox[o, j, m, i].astype(F32)
+            result[:, columns(2 * j + i)] = both.astype(BF16)
 
     def sum_a(o, j):
+        if (o, j) in PAIR_FIRST:
+            for m, at in ((3, 7), (1, 4), (2, 5), (0, 1)):
+                post(o, j, at, m, y_far)
+            return
         post(o, j, 6, 0, x_up)
         post(o, j, 7, 1, x_down)
         post(o, j, 4, 2, x_up)
         post(o, j, 3, 3, x_down)
 
     def sum_b(o, j):
+        if (o, j) in PAIR_FIRST:
+            collect(o, j, 3)
+            for i, device in ((0, x_up), (1, x_down)):
+                add(o, j, 6, 3, i)
+                send(
+                    part.at[o, 2 * j + i, 6], inbox.at[o, j, 4, i], rs_send.at[o, j, 4 + 3 * i],
+                    rs_recv.at[o, j, 4 + 3 * i], device,
+                )
+            for m, at in ((1, 2), (2, 3)):
+                collect(o, j, m)
+                for i in range(2):
+                    add(o, j, at, m, i)
+            return
         for m, at, device in ((0, 2, x_up), (1, 5, x_down)):
             collect(o, j, m)
             for i in range(2):
-                both = part[o, 2 * j + i, at].astype(F32) + inbox[o, j, m, i].astype(F32)
-                part[o, 2 * j + i, at] = both.astype(BF16)
+                add(o, j, at, m, i)
             post(o, j, at, 4 + m, device)
 
     def sum_c(o, j):
+        if (o, j) in PAIR_FIRST:
+            for i, at, device in ((0, 2, x_up), (1, 3, x_down)):
+                arrived(inbox.at[o, j, 4, i], rs_recv.at[o, j, 4 + 3 * i], sibling)
+                add(o, j, at, 4, i)
+                post(o, j, at, 5 + i, device)
+            return
         for m in (2, 3, 4, 5):
             collect(o, j, m)
         for i in range(2):
@@ -363,67 +375,75 @@
         post(o, j, 1, 6, y_far)
 
     def sum_d(o, j):
+        if (o, j) in PAIR_FIRST:
+            for m in (0, 5, 6):
+                collect(o, j, m)
+            finish(o, j, (0, 5, 6))
+            return
         collect(o, j, 6)
-        result = out_ref if o == 0 else ig_ref
-        for i in range(2):
-            both = part[o, 2 * j + i, 0].astype(F32) + inbox[o, j, 3, i].astype(F32)
-            both = both + inbox[o, j, 4, i].astype(F32)
-            result[:, columns(2 * j + i)] = (both + inbox[o, j, 6, i].astype(F32)).astype(BF16)
-
+        finish(o, j, (3, 4, 6))
+
+    relay_own(GATE)
+    relay_own(TOK)
+    second(TOK)
+    second(GATE)
+    relay_own(UP)
+    relay_other(TOK)
+    relay_other(GATE)
+    second(UP)
+    relay_own(GRAD)
+    second(GRAD)
+    for k in range(1, SLOTS):
+        need(TOK, k)
+    for k in (2, 3):
+        need(GATE, k)
+        need(UP, k)
     forward(0)
-    second(DOWN)
     forward(1)
-    fourth(GRAD)
-    fourth(UP)
-    third(DOWN)
-    fifth(GATE)
+    relay_other(UP)
+    start(DOWN)
+    relay_other(GRAD)
     forward(2)
-    fifth(GRAD)
-    sixth(GRAD)
-    fifth(UP)
-    sixth(GATE)
-    sixth(UP)
     forward(3)
     arrived(keep_buf.at[1], core_recv.at[3, 0], sibling)
     activate()
-    from_sibling(DOWN, 0)
-    from_sibling(DOWN, 1)
+    second(DOWN)
+    relay_own(DOWN)
+    for k in range(1, SLOTS):
+        need(GRAD, k)
+    ready(0)
     out_part(0)
     sum_a(0, 0)
     backward(0)
-    from_sibling(DOWN, 2)
-    from_sibling(DOWN, 3)
+    ready(1)
     out_part(1)
     sum_a(0, 1)
     sum_b(0, 0)
     backward(1)
-    fourth(DOWN)
-    from_sibling(DOWN, 4)
-    from_sibling(DOWN, 5)
+    relay_other(DOWN)
+    sum_b(0, 1)
+    sum_c(0, 0)
+    sum_c(0, 1)
+    ready(2)
     out_part(2)
     sum_a(0, 2)
-    sum_b(0, 1)
-    sum_c(0, 0)
     backward(2)
-    fifth(DOWN)
+    sum_d(0, 0)
+    ready(3)
+    out_part(3)
+    sum_a(0, 3)
+    backward(3)
     sum_b(0, 2)
-    sum_c(0, 1)
-    sum_d(0, 0)
-    sixth(DOWN)
-    from_sibling(DOWN, 6)
-    from_sibling(DOWN, 7)
-    backward(3)
+    sum_d(0, 1)
     pull_back()
     grad_part(0)
     sum_a(1, 0)
-    out_part(3)
-    sum_a(0, 3)
+    sum_b(0, 3)
     sum_c(0, 2)
-    sum_d(0, 1)
     grad_part(1)
     sum_a(1, 1)
     sum_b(1, 0)
-    sum_b(0, 3)
+    sum_c(0, 3)
     grad_part(2)
     sum_a(1, 2)
     sum_b(1, 1)
@@ -431,11 +451,10 @@
     sum_d(0, 2)
     grad_part(3)
     sum_a(1, 3)
-    sum_c(0, 3)
+    sum_d(0, 3)
     sum_b(1, 2)
     sum_c(1, 1)
     sum_d(1, 0)
-    sum_d(0, 3)
     sum_b(1, 3)
     sum_c(1, 2)
     sum_d(1, 1)
@@ -480,12 +499,12 @@
             pltpu.VMEM((2, SLOTS, SLOTS, chunk, width), BF16),
             pltpu.VMEM((2, PAIRS, 7, 2, chunk, width), BF16),
             dma((6,)),
-            dma((5, 9)),
-            dma((5, SLOTS + 2)),
+            dma((5, 14)),
+            dma((5, 2 * SLOTS)),
             dma((4, SLOTS)),
             dma((4, SLOTS)),
-            dma((2, PAIRS, 7)),
-            dma((2, PAIRS, 7)),
+            dma((2, PAIRS, 8)),
+            dma((2, PAIRS, 8)),
         ],
         compiler_params=pltpu.CompilerParams(
             collective_id=0, has_side_effects=True, vmem_limit_bytes=64_000_000

time: 196 us -> 163 us (0.83)
  Pallas kernels: 189 us -> 156 us
    pallas_call x1, Pallas kernels: 189 us -> 156 us  [local(): pl.pallas_call(kernel, out_shape=[jax.ShapeDtypeStruct((chunk, model), BF...]
where the time goes in v2:
time: 163 us
  Pallas kernels  156 us (96%)
  local copies, waits for them, and re-layouts  4.68 us (3%)
    pallas_call x1, Pallas kernels, local(): pl.pallas_call(kernel, out_shape=[jax.ShapeDtypeStruct((chunk, model), BF...  156 us
    unnamed x10, local copies, waits for them, and re-layouts  3.96 us

profile of v2, /device:TPU:0, one launch (start us, length us, event | category | flops | bytes accessed | tf_op | source)
XLA Modules:
  0.0 162.6 jit_solution(5098572721052085602)
XLA Ops:
  0.7 0.0 copy-start.2
  0.7 0.0 copy-start.3
  0.7 0.6 copy-done.2
  1.3 0.0 copy-done.3
  1.4 0.0 copy-start.1
  1.4 0.7 copy-done.1
  2.1 0.1 reshape.32
  2.1 0.6 gather_fusion
  2.7 0.1 broadcast_select_fusion
  2.8 0.1 select_n.52
  2.9 0.8 fusion.onehot_ref
  3.6 156.3 %swiglu.1 = (bf16[56,4096]{1,0:T(8,128)(2,1)}, bf16[56,4096]{1,0:T(8,128)(2,1)}) custom-call(s32[8,7]{1,0:T(8,128)} %keep_ref.1, bf16[56,4096]{1,0:T(8,128)(2,1)} %tok_ref.1, bf16[56,4096]{1,0:T(8,128)(2,1)} %grad_ref.1, bf16[512,896]{1,0:T(8,128)(2,1)} %gate_ref.1, bf16[512,896]{1,0:T(8,128)(2,1)} %up_ref.1, bf16[896,512]{1,0:T(8,128)(2,1)} %down_ref.1, ...), custom_call_target="tpu_custom_call" | custom-call | tf_op jit(solution)/shard_map/swiglu/pallas_call | solution.py:484
  160.0 0.0 copy-start
  160.0 1.9 %copy.13 = bf16[56,4096]{1,0:T(8,128)(2,1)} copy(bf16[56,4096]{1,0:T(8,128)(2,1)} %get-tuple-element.6) | data formatting | bytes 917504
  161.9 0.0 copy-done
  161.9 0.8 copy.14
  (2 shorter events, 0.0 us)
Async XLA Ops:
  0.7 0.7 copy-start.2
  0.7 0.7 copy-start.3
  1.4 0.7 copy-start.1
  160.0 1.9 %copy-start = (bf16[56,4096]{1,0:T(8,128)(2,1)S(1)}, bf16[56,4096]{1,0:T(8,128)(2,1)}, u32[]{:S(2)}) copy-start(bf16[56,4096]{1,0:T(8,128)(2,1)} %get-tuple-element.7) | copy-start | bytes 1376260
